TPU v7x, 256 devices: a whole 4x4x8 slice. The times are simulated.
256 devices in a mesh: pipe: 2 (over core), obs: 16 (over y, x), patch: 8 (over z).
Axes of the slice: x: 4, y: 4, z: 8, core: 2. Of those that a mesh axis runs over, the one named last changes fastest.
Arguments:
- patch_tokens: bfloat16 [4096, 2048], P('patch', 'obs'), may hold values from -40 to 40
- obs_tokens: bfloat16 [2048, 2048], P('patch', 'obs'), may hold values from -40 to 40
- footprint: int32 [32, 8], P('patch'), may hold values from 0 to 15, as said below
- list_counts: int32 [32], P('patch'), may hold values from 1 to 8
- footprint_bias: float32 [32, 8], P('patch'), may hold values from -4 to 290
- w_query: bfloat16 [2, 2048, 2048], P('pipe', None, 'obs'), may hold values from -0.125 to 0.125
- w_key: bfloat16 [2, 2048, 2048], P('pipe', None, 'obs'), may hold values from -0.125 to 0.125
- w_value: bfloat16 [2, 2048, 2048], P('pipe', None, 'obs'), may hold values from -0.125 to 0.125
- w_out: bfloat16 [2, 2048, 2048], P('pipe', 'obs'), may hold values from -0.125 to 0.125
- patch_gain: float32 [2, 2048], P('pipe'), may hold values from 0.1 to 1.9
- obs_gain: float32 [2, 2048], P('pipe'), may hold values from 0.1 to 1.9
Outputs:
- sections: bfloat16 [2, 4096, 2048], P('pipe', 'patch', 'obs')
Inputs may be any that keep to these rules, and one draw needn't show every extreme that they name: `footprint`: entries are global observation block indices. In each row the first list_counts entries (the live ones) are distinct, the rest are to be ignored. For a device along patch and any device along patch, all live entries of the first device's rows that lie in the second device's range of 2 blocks name one and the same block.
All inputs are finite; a program needn't handle non-finite values.
Results may differ from a plain program's by a relative error of at most 0.012.
Values may be sent and summed in bfloat16 or wider, within the bound.
No kernel may reach another device: no remote copies, remote signals or barrier semaphores. Data moves between devices by JAX's collectives and lax.ppermute only.
A program may use at most 64 MiB of HBM per device.

v0:
```python
import jax
import jax.numpy as jnp
from jax import lax
from jax.sharding import PartitionSpec as P

HS = 128
BLK = 128
MB = 128


def passed_along(value, axis, steps):
    count = lax.axis_size(axis)
    first, last = (max(0, -steps), min(count, count - steps))
    return lax.ppermute(value, axis, [(source, source + steps) for source in range(first, last)])


def rms_round(values, gain):
    widened = values.astype(jnp.float32)
    scaled = widened * lax.rsqrt(jnp.mean(widened * widened, axis=-1, keepdims=True) + 1e-05)
    return (scaled * gain).astype(jnp.bfloat16)


def store_rows(sections, out_piece, is_valid, row_start):
    current = lax.dynamic_slice_in_dim(sections, row_start, out_piece.shape[0], 1)
    kept = jnp.where(is_valid, out_piece[None], current)
    return lax.dynamic_update_slice_in_dim(sections, kept, row_start, 1)


def on_device(
    patch_tokens,
    obs_tokens,
    footprint,
    list_counts,
    footprint_bias,
    w_query,
    w_key,
    w_value,
    w_out,
    patch_gain,
    obs_gain,
):
    pipe_segment = lax.axis_index("pipe")
    segment_count = lax.axis_size("pipe")
    obs_column = lax.axis_index("obs")
    feature_part = patch_tokens.shape[1]
    full_features = feature_part * lax.axis_size("obs")
    head_width = w_query.shape[2]
    heads_here = head_width // HS
    list_slots = footprint.shape[1]
    micro_count = patch_tokens.shape[0] // MB
    blocks_micro = MB // BLK
    score_scale = HS ** (-0.5)
    observed = lax.all_gather(obs_tokens, "obs", axis=1, tiled=True)
    obs_normed = rms_round(observed, obs_gain[0])
    key_values = jnp.concatenate(
        [
            jnp.dot(obs_normed, w_key[0], preferred_element_type=jnp.float32).astype(jnp.bfloat16),
            jnp.dot(obs_normed, w_value[0], preferred_element_type=jnp.float32).astype(
                jnp.bfloat16
            ),
        ],
        axis=1,
    )
    local_blocks = key_values.reshape(-1, BLK, 2 * head_width)
    kv_table = lax.all_gather(local_blocks, "patch", axis=0, tiled=True)

    def attend_block(segment_input, micro_index):
        patch_normed = rms_round(segment_input, patch_gain[0])
        queries = (
            jnp.dot(patch_normed, w_query[0], preferred_element_type=jnp.float32) * score_scale
        ).astype(jnp.bfloat16)
        queries = queries.reshape(blocks_micro, BLK, heads_here, HS)
        first_block = micro_index * blocks_micro
        slot_part = lax.dynamic_slice_in_dim(footprint, first_block, blocks_micro, 0)
        count_part = lax.dynamic_slice_in_dim(list_counts, first_block, blocks_micro, 0)
        bias_part = lax.dynamic_slice_in_dim(footprint_bias, first_block, blocks_micro, 0)
        picked = kv_table[slot_part].reshape(blocks_micro, list_slots * BLK, 2 * head_width)
        key_part = picked[:, :, :head_width].reshape(blocks_micro, list_slots * BLK, heads_here, HS)
        value_part = picked[:, :, head_width:].reshape(
            blocks_micro, list_slots * BLK, heads_here, HS
        )
        scores = jnp.einsum(
            "bqhd,bkhd->bhqk", queries, key_part, preferred_element_type=jnp.float32
        )
        alive_mask = jnp.repeat(jnp.arange(list_slots)[None, :] < count_part[:, None], BLK, axis=1)
        added = jnp.repeat(bias_part, BLK, axis=1)
        scores = jnp.where(alive_mask[:, None, None, :], scores + added[:, None, None, :], -1e30)
        row_max = jnp.max(scores, axis=-1, keepdims=True)
        weights = jnp.exp(scores - row_max)
        weights = (weights / jnp.sum(weights, axis=-1, keepdims=True)).astype(jnp.bfloat16)
        context = jnp.einsum(
            "bhqk,bkhd->bqhd", weights, value_part, preferred_element_type=jnp.float32
        ).astype(jnp.bfloat16)
        context = context.reshape(MB, head_width)
        return jnp.dot(context, w_out[0], preferred_element_type=jnp.float32)

    def spare_block(segment_input, micro_index):
        return jnp.zeros((MB, full_features), jnp.float32)

    tick_total = micro_count + segment_count - 1
    sections = jnp.zeros((1, patch_tokens.shape[0], feature_part), jnp.bfloat16)
    rows_all = lax.all_gather(patch_tokens, "obs", axis=1, tiled=True)
    arriving = jnp.zeros((MB, full_features), jnp.bfloat16)
    for tick_num in range(tick_total):
        tick_micro = tick_num - pipe_segment
        is_valid = (tick_micro >= 0) & (tick_micro < micro_count)
        micro_index = jnp.clip(tick_micro, 0, micro_count - 1)
        own_rows = lax.dynamic_slice_in_dim(rows_all, micro_index * MB, MB, 0)
        segment_input = jnp.where(pipe_segment == 0, own_rows, arriving)
        partial_value = lax.cond(is_valid, attend_block, spare_block, segment_input, micro_index)
        head_total = lax.psum(partial_value.astype(jnp.bfloat16), "obs").astype(jnp.float32)
        segment_output = (segment_input.astype(jnp.float32) + head_total).astype(jnp.bfloat16)
        out_piece = lax.dynamic_slice_in_dim(
            segment_output, obs_column * feature_part, feature_part, 1
        )
        sections = store_rows(sections, out_piece, is_valid, micro_index * MB)
        if tick_num + 1 < tick_total:
            arriving = passed_along(segment_output, "pipe", 1)
    return sections


def solution(mesh):
    in_specs = (
        P("patch", "obs"),
        P("patch", "obs"),
        P("patch", None),
        P("patch"),
        P("patch", None),
        P("pipe", None, "obs"),
        P("pipe", None, "obs"),
        P("pipe", None, "obs"),
        P("pipe", "obs", None),
        P("pipe", None),
        P("pipe", None),
    )
    out_specs = P("pipe", "patch", "obs")
    return jax.shard_map(
        on_device, mesh=mesh, in_specs=in_specs, out_specs=out_specs, check_vma=False
    )
```

profile of v0, /device:TPU:2, one launch (start us, length us, event | category | flops | bytes accessed | tf_op | source)
XLA Modules:
  0.0 700.2 jit_solution(2485516238832570236)
XLA Ops:
  8.1 52.5 %all-gather.6.cloned.1.call-done = bf16[256,2048]{1,0:T(8,128)(2,1)} async-done(((bf16[256,128]{1,0:T(8,128)(2,1)}), bf16[256,2048]{1,0:T(8,128)(2,1)}) %all-gather.6.cloned.1.call-update) | async-done | bytes 1048592 | tf_op jit(solution)/shard_map/all_gather | solution.py:53
  60.6 1.6 fusion.120
  62.2 1.8 convolution_convert_fusion.5
  65.5 48.9 %all-gather.4.cloned.1.call-done = bf16[512,2048]{1,0:T(8,128)(2,1)} async-done(((bf16[512,128]{1,0:T(8,128)(2,1)}), bf16[512,2048]{1,0:T(8,128)(2,1)}) %all-gather.4.cloned.1.call-update) | async-done | bytes 2097168 | tf_op jit(solution)/shard_map/all_gather | solution.py:102
  114.4 1.1 dynamic-slice_select_fusion.4
  115.6 38.8 %all-gather.8.cloned.1.call-done = bf16[16,128,256]{2,1,0:T(8,128)(2,1)} async-done(((bf16[2,128,256]{2,1,0:T(8,128)(2,1)}), bf16[16,128,256]{2,1,0:T(8,128)(2,1)}) %all-gather.8.cloned.1.call-update) | async-done | bytes 1048592 | tf_op jit(solution)/shard_map/all_gather | solution.py:65
  154.4 6.1 conditional.5
  154.5 1.8 gather_fusion
  158.7 1.8 fusion.3
  161.4 93.9 %all-reduce.6.cloned.1.call-done = bf16[128,2048]{1,0:T(8,128)(2,1)} async-done(((bf16[128,2048]{1,0:T(8,128)(2,1)}), bf16[128,2048]{1,0:T(8,128)(2,1)}) %all-reduce.6.cloned.1.call-update) | async-done | bytes 524304 | tf_op jit(solution)/shard_map/psum | solution.py:111
  255.3 2.1 add_convert_fusion.3
  257.5 1.3 collective-permute-start
  258.8 1.7 collective-permute-done
  260.5 1.2 dynamic-slice_select_fusion.3
  261.7 6.7 conditional.6
  264.6 1.6 fusion.138
  266.5 1.9 fusion.27
  268.4 0.8 copy-done.3
  269.3 95.4 %all-reduce.8.cloned.1.call-done = bf16[128,2048]{1,0:T(8,128)(2,1)} async-done(((bf16[128,2048]{1,0:T(8,128)(2,1)}), bf16[128,2048]{1,0:T(8,128)(2,1)}) %all-reduce.8.cloned.1.call-update) | async-done | bytes 524304 | tf_op jit(solution)/shard_map/psum | solution.py:111
  364.6 1.2 add_convert_fusion.2
  365.8 1.3 collective-permute-start.1
  367.1 1.5 collective-permute-done.1
  368.6 1.2 dynamic-slice_select_fusion.2
  369.8 7.7 %conditional.7 = (bf16[128,2048]{1,0:T(8,128)(2,1)S(1)}) conditional(s32[]{:T(128)} %convert_element_type.212, () %tuple.39, (s32[]{:T(128)}, s32[4,8]{1,0:T(4,128)S(1)}, bf16[16,128,256]{2,1,0:T(8,128)(2,1)S(1)}, s32[4]{0:T(128)S(1)}, bf16[128,2048]{1,0:T(8,128)(2,1)S(1)}, /*index=5*/f32[1,2048]{1,0:T(1,128)S(1)}, ...), branch_computations={%region_13.14_spmd, %region_14.18_spmd} | conditional | flops 204260256 | bytes 7891790 | solution.py:110
  369.9 1.4 gather_fusion.2
  372.7 1.7 fusion.143
  374.4 0.8 copy-done.10
  375.4 2.0 fusion.51
  377.5 0.8 copy-done.4
  378.4 95.4 %all-reduce.10.cloned.1.call-done = bf16[128,2048]{1,0:T(8,128)(2,1)} async-done(((bf16[128,2048]{1,0:T(8,128)(2,1)}), bf16[128,2048]{1,0:T(8,128)(2,1)}) %all-reduce.10.cloned.1.call-update) | async-done | bytes 524304 | tf_op jit(solution)/shard_map/psum | solution.py:111
  473.7 1.2 add_convert_fusion.1
  474.9 2.1 collective-permute-start.2
  477.0 0.8 collective-permute-done.2
  477.9 1.2 dynamic-slice_select_fusion.1
  479.1 7.8 %conditional.8 = (bf16[128,2048]{1,0:T(8,128)(2,1)S(1)}) conditional(s32[]{:T(128)} %convert_element_type.217, () %tuple.41, (s32[]{:T(128)}, s32[4,8]{1,0:T(4,128)S(1)}, bf16[16,128,256]{2,1,0:T(8,128)(2,1)S(1)}, s32[4]{0:T(128)S(1)}, bf16[128,2048]{1,0:T(8,128)(2,1)S(1)}, /*index=5*/f32[1,2048]{1,0:T(1,128)S(1)}, ...), branch_computations={%region_19.20_spmd, %region_20.24_spmd} | conditional | flops 204260256 | bytes 7891790 | solution.py:110
  479.2 1.4 gather_fusion.3
  482.1 1.7 fusion.148
  483.9 0.8 copy-done.11
  484.9 2.0 fusion.75
  486.9 0.8 copy-done.5
  487.8 95.6 %all-reduce.12.cloned.1.call-done = bf16[128,2048]{1,0:T(8,128)(2,1)} async-done(((bf16[128,2048]{1,0:T(8,128)(2,1)}), bf16[128,2048]{1,0:T(8,128)(2,1)}) %all-reduce.12.cloned.1.call-update) | async-done | bytes 524304 | tf_op jit(solution)/shard_map/psum | solution.py:111
  583.3 1.2 add_convert_fusion
  584.5 2.1 collective-permute-start.3
  586.6 0.8 collective-permute-done.3
  587.5 1.2 dynamic-slice_select_fusion
  590.4 0.8 fusion.131
  591.2 100.7 %all-reduce.14.cloned.1.call-done = bf16[128,2048]{1,0:T(8,128)(2,1)} async-done(((bf16[128,2048]{1,0:T(8,128)(2,1)}), bf16[128,2048]{1,0:T(8,128)(2,1)}) %all-reduce.14.cloned.1.call-update) | async-done | bytes 524304 | tf_op jit(solution)/shard_map/psum | solution.py:111
  691.9 1.4 fusion.129
  (105 shorter events, 15.0 us)
Async XLA Ops:
  6.5 55.6 %copy-start = (bf16[1,2048,128]{2,1,0:T(8,128)(2,1)S(1)}, bf16[1,2048,128]{2,1,0:T(8,128)(2,1)}, u32[]{:S(2)}) copy-start(bf16[1,2048,128]{2,1,0:T(8,128)(2,1)} %param.28) | copy-start | bytes 1572868
  6.5 57.4 %copy-start.16 = (f32[1,2048]{1,0:T(1,128)S(1)}, f32[1,2048]{1,0:T(1,128)}, u32[]{:S(2)}) copy-start(f32[1,2048]{1,0:T(1,128)} %param.31) | copy-start | bytes 24580
  6.5 57.4 %copy-start.13 = (bf16[1,2048,128]{2,1,0:T(8,128)(2,1)S(1)}, bf16[1,2048,128]{2,1,0:T(8,128)(2,1)}, u32[]{:S(2)}) copy-start(bf16[1,2048,128]{2,1,0:T(8,128)(2,1)} %param.27) | copy-start | bytes 1572868
  6.5 54.0 %all-gather.6.cloned.1.call-start = ((), (), s32[]{:S(2)}) async-start(), calls=%async_computation.1 | async-start | bytes 1114112 | tf_op jit(solution)/shard_map/all_gather | solution.py:53
  7.3 107.2 %all-gather.4.cloned.1.call-start = ((), (), s32[]{:S(2)}) async-start(), calls=%async_computation | async-start | bytes 2228224 | tf_op jit(solution)/shard_map/all_gather | solution.py:102
  8.0 146.4 %all-gather.8.cloned.1.call-start = ((), (), s32[]{:S(2)}) async-start(), calls=%async_computation.2 | async-start | bytes 1179648 | tf_op jit(solution)/shard_map/all_gather | solution.py:65
  60.5 3.4 copy-start.7
  64.0 90.4 %copy-start.14 = (bf16[1,2048,128]{2,1,0:T(8,128)(2,1)S(1)}, bf16[1,2048,128]{2,1,0:T(8,128)(2,1)}, u32[]{:S(2)}) copy-start(bf16[1,2048,128]{2,1,0:T(8,128)(2,1)} %param.26) | copy-start | bytes 1572868
  64.0 90.4 %copy-start.17 = (f32[1,2048]{1,0:T(1,128)S(1)}, f32[1,2048]{1,0:T(1,128)}, u32[]{:S(2)}) copy-start(f32[1,2048]{1,0:T(1,128)} %param.30) | copy-start | bytes 24580
  64.0 90.4 %copy-start.18 = (s32[4,8]{1,0:T(4,128)S(1)}, s32[4,8]{1,0:T(4,128)}, u32[]{:S(2)}) copy-start(s32[4,8]{1,0:T(4,128)} %param.23) | copy-start | bytes 388
  64.0 90.4 %copy-start.19 = (f32[4,8]{1,0:T(4,128)S(1)}, f32[4,8]{1,0:T(4,128)}, u32[]{:S(2)}) copy-start(f32[4,8]{1,0:T(4,128)} %param.25) | copy-start | bytes 388
  64.0 90.3 %copy-start.20 = (s32[4]{0:T(128)S(1)}, s32[4]{0:T(128)}, u32[]{:S(2)}) copy-start(s32[4]{0:T(128)} %param.24) | copy-start | bytes 52
  65.4 189.9 %all-reduce.6.cloned.1.call-start = ((), (), s32[]{:S(2)}) async-start(), calls=%async_computation.3 | async-start | bytes 1048576 | tf_op jit(solution)/shard_map/psum | solution.py:111
  160.5 0.8 copy-start.2
  160.5 101.1 %copy-start.1 = (bf16[16,128,256]{2,1,0:T(8,128)(2,1)S(1)}, bf16[16,128,256]{2,1,0:T(8,128)(2,1)}, u32[]{:S(2)}) copy-start(bf16[16,128,256]{2,1,0:T(8,128)(2,1)} %all-gather.8.cloned.1.call-done) | copy-start | bytes 3145732
  161.3 203.3 %all-reduce.8.cloned.1.call-start = ((), (), s32[]{:S(2)}) async-start(), calls=%async_computation.4 | async-start | bytes 1048576 | tf_op jit(solution)/shard_map/psum | solution.py:111
  257.5 3.0 collective-permute-start
  261.7 0.8 copy-start.15
  263.1 3.1 copy-start.12
  268.4 0.8 copy-start.3
  269.2 204.5 %all-reduce.10.cloned.1.call-start = ((), (), s32[]{:S(2)}) async-start(), calls=%async_computation.5 | async-start | bytes 1048576 | tf_op jit(solution)/shard_map/psum | solution.py:111
  365.8 2.8 collective-permute-start.1
  374.4 0.8 copy-start.10
  377.5 0.8 copy-start.4
  378.3 205.0 %all-reduce.12.cloned.1.call-start = ((), (), s32[]{:S(2)}) async-start(), calls=%async_computation.6 | async-start | bytes 1048576 | tf_op jit(solution)/shard_map/psum | solution.py:111
  474.9 4.1 copy-start.8
  474.9 2.9 collective-permute-start.2
  483.8 0.8 copy-start.11
  486.9 0.8 copy-start.5
  487.7 204.2 %all-reduce.14.cloned.1.call-start = ((), (), s32[]{:S(2)}) async-start(), calls=%async_computation.7 | async-start | bytes 1048576 | tf_op jit(solution)/shard_map/psum | solution.py:111
  584.5 2.9 collective-permute-start.3
  588.7 0.8 copy-start.6
  591.2 100.7 %copy-start.9 = (bf16[1,512,128]{2,1,0:T(8,128)(2,1)}, bf16[1,512,128]{2,1,0:T(8,128)(2,1)S(1)}, u32[]{:S(2)}) copy-start(bf16[1,512,128]{2,1,0:T(8,128)(2,1)S(1)} %fusion.130) | copy-start | bytes 393220
Sparse Core Ops, SparseCore 0:
  9.7 50.7 all-gather.5
  63.0 51.4 all-gather.3
  116.2 38.1 all-gather.7
  161.4 93.8 all-reduce.5
  269.3 95.2 all-reduce.7
  378.4 95.2 all-reduce.9
  487.9 95.4 all-reduce.11
  589.6 102.2 all-reduce.13
where the time goes:
time: 701 us; the launch traced here: 700 us
  waiting for transfers between devices  628 us (90%)
  other arithmetic  20.3 us (3%)
  matrix products  15.8 us (2%)
  local copies, waits for them, and re-layouts  15.4 us (2%)
  between operations  13.8 us (2%)
  starting transfers between devices  7.12 us (1%)
    psum x5, waiting for transfers between devices, on_device(): lax.psum(partial_value.astype(jnp.bfloat16), 'obs').astype(jnp.float32)  481 us
    all_gather x1, waiting for transfers between devices, on_device(): observed = lax.all_gather(obs_tokens, 'obs', axis=1, tiled=True)  52.5 us
    all_gather x1, waiting for transfers between devices, on_device(): rows_all = lax.all_gather(patch_tokens, 'obs', axis=1, tiled=True)  48.9 us
    all_gather x1, waiting for transfers between devices, on_device(): kv_table = lax.all_gather(local_blocks, 'patch', axis=0, tiled=True)  38.8 us
  transfers between devices with their start and end apart: 12, of which 12 were waited for; matrix products, arithmetic and copies ran while one was open for 1% of the time, Pallas kernels for 0%

commit v1 on v0

--- a/solution.py
+++ b/solution.py
@@ -6,6 +6,22 @@
 HS = 128
 BLK = 128
 MB = 128
+
+
+def ring_gather(x, axis, dim):
+    ways, here, step = (lax.axis_size(axis), lax.axis_index(axis), x.shape[dim])
+    shape = [n * ways if d == dim else n for d, n in enumerate(x.shape)]
+    full = lax.dynamic_update_slice_in_dim(jnp.zeros(shape, x.dtype), x, here * step, axis=dim)
+    going_up = going_down = x
+    for far in range(1, ways // 2 + 1):
+        going_up = lax.ppermute(going_up, axis, [(d, (d + 1) % ways) for d in range(ways)])
+        full = lax.dynamic_update_slice_in_dim(full, going_up, (here - far) % ways * step, axis=dim)
+        if 2 * far < ways:
+            going_down = lax.ppermute(going_down, axis, [(d, (d - 1) % ways) for d in range(ways)])
+            full = lax.dynamic_update_slice_in_dim(
+                full, going_down, (here + far) % ways * step, axis=dim
+            )
+    return full
 
 
 def passed_along(value, axis, steps):
@@ -50,7 +66,7 @@
     micro_count = patch_tokens.shape[0] // MB
     blocks_micro = MB // BLK
     score_scale = HS ** (-0.5)
-    observed = lax.all_gather(obs_tokens, "obs", axis=1, tiled=True)
+    observed = ring_gather(obs_tokens, "obs", 1)
     obs_normed = rms_round(observed, obs_gain[0])
     key_values = jnp.concatenate(
         [

time: 701 us -> 655 us (0.934)
  waiting for transfers between devices: 628 us -> 549 us
  starting transfers between devices: 7.12 us -> 41.7 us
    all_gather x1 -> x0, waiting for transfers between devices: 52.5 us -> none  [on_device(): observed = lax.all_gather(obs_tokens, 'obs', axis=1, tiled=True)]
    all_gather x1, waiting for transfers between devices: 48.9 us -> 0.02 us  [on_device(): rows_all = lax.all_gather(patch_tokens, 'obs', axis=1, tiled=True)]
    ppermute x0 -> x15, starting transfers between devices: none -> 34.6 us  [the longest x7 31.7 us: ring_gather(): lax.ppermute(going_down, axis, [(d, (d - 1) % ways) for d in range(ways)])]
    ppermute x0 -> x15, waiting for transfers between devices: none -> 24.2 us  [the longest x8 24.2 us: ring_gather(): lax.ppermute(going_up, axis, [(d, (d + 1) % ways) for d in range(ways)])]
  transfers between devices with their start and end apart: 12 -> 26, of which waited for: 12 -> 18; matrix products, arithmetic and copies ran while one was open for 1% -> 1% of each run, Pallas kernels for 0% -> 0%
where the time goes in v1:
time: 655 us; the launch traced here: 653 us
  waiting for transfers between devices  549 us (84%)
  starting transfers between devices  41.7 us (6%)
  other arithmetic  18.1 us (3%)
  local copies, waits for them, and re-layouts  15.8 us (2%)
  matrix products  14.6 us (2%)
  between operations  13.9 us (2%)
    psum x5, waiting for transfers between devices, on_device(): lax.psum(partial_value.astype(jnp.bfloat16), 'obs').astype(jnp.float32)  481 us
    all_gather x1, waiting for transfers between devices, on_device(): kv_table = lax.all_gather(local_blocks, 'patch', axis=0, tiled=True)  38.7 us
    ppermute x7, starting transfers between devices, ring_gather(): lax.ppermute(going_down, axis, [(d, (d - 1) % ways) for d in range(ways)])  31.7 us
    ppermute x8, waiting for transfers between devices, ring_gather(): lax.ppermute(going_up, axis, [(d, (d + 1) % ways) for d in range(ways)])  24.2 us
  transfers between devices with their start and end apart: 26, of which 18 were waited for; matrix products, arithmetic and copies ran while one was open for 1% of the time, Pallas kernels for 0%

profile of v1, /device:TPU:2, one launch (start us, length us, event | category | flops | bytes accessed | tf_op | source)
XLA Modules:
  0.0 653.5 jit_solution(7598545366572140734)
XLA Ops:
  7.3 1.6 collective-permute-start
  10.7 1.4 collective-permute-done
  12.1 1.3 collective-permute-start.2
  13.4 4.1 collective-permute-start.3
  17.5 2.2 collective-permute-done.2
  19.7 5.3 collective-permute-start.5
  25.1 2.6 collective-permute-done.4
  27.7 5.5 collective-permute-start.7
  33.2 2.8 collective-permute-done.6
  36.0 5.2 collective-permute-start.9
  41.2 2.2 collective-permute-done.8
  43.4 5.3 collective-permute-start.11
  48.8 3.3 collective-permute-done.10
  52.1 5.5 collective-permute-start.13
  57.7 2.5 collective-permute-done.12
  60.3 7.2 %collective-permute-done.14 = bf16[256,128]{1,0:T(8,128)(2,1)S(1)} collective-permute-done((bf16[256,128]{1,0:T(8,128)(2,1)S(1)}, bf16[256,128]{1,0:T(8,128)(2,1)S(1)}, u32[]{:S(2)}, u32[]{:S(2)}) %collective-permute-start.14) | collective-permute-done | bytes 65568 | tf_op jit(solution)/shard_map/ppermute | solution.py:17
  71.1 38.7 %all-gather.5.cloned.1.call-done = bf16[16,128,256]{2,1,0:T(8,128)(2,1)} async-done(((bf16[2,128,256]{2,1,0:T(8,128)(2,1)}), bf16[16,128,256]{2,1,0:T(8,128)(2,1)}) %all-gather.5.cloned.1.call-update) | async-done | bytes 1048592 | tf_op jit(solution)/shard_map/all_gather | solution.py:81
  109.8 6.1 conditional.5
  110.0 1.8 gather_fusion
  114.2 1.8 fusion.3
  116.8 93.8 %all-reduce.6.cloned.1.call-done = bf16[128,2048]{1,0:T(8,128)(2,1)} async-done(((bf16[128,2048]{1,0:T(8,128)(2,1)}), bf16[128,2048]{1,0:T(8,128)(2,1)}) %all-reduce.6.cloned.1.call-update) | async-done | bytes 524304 | tf_op jit(solution)/shard_map/psum | solution.py:127
  210.6 1.4 add_convert_fusion.3
  212.0 1.3 collective-permute-start.15
  213.4 1.5 collective-permute-done.15
  214.8 1.2 dynamic-slice_select_fusion.3
  216.0 5.9 conditional.6
  218.2 1.6 fusion.138
  220.0 1.9 fusion.27
  222.8 95.3 %all-reduce.8.cloned.1.call-done = bf16[128,2048]{1,0:T(8,128)(2,1)} async-done(((bf16[128,2048]{1,0:T(8,128)(2,1)}), bf16[128,2048]{1,0:T(8,128)(2,1)}) %all-reduce.8.cloned.1.call-update) | async-done | bytes 524304 | tf_op jit(solution)/shard_map/psum | solution.py:127
  319.3 1.3 collective-permute-start.16
  320.6 1.5 collective-permute-done.16
  322.1 1.2 dynamic-slice_select_fusion.2
  323.3 7.7 %conditional.7 = (bf16[128,2048]{1,0:T(8,128)(2,1)S(1)}) conditional(s32[]{:T(128)} %convert_element_type.212, () %tuple.39, (s32[]{:T(128)}, s32[4,8]{1,0:T(4,128)S(1)}, bf16[16,128,256]{2,1,0:T(8,128)(2,1)S(1)}, s32[4]{0:T(128)S(1)}, bf16[128,2048]{1,0:T(8,128)(2,1)S(1)}, /*index=5*/f32[1,2048]{1,0:T(1,128)S(1)}, ...), branch_computations={%region_13.14_spmd, %region_14.18_spmd} | conditional | flops 204260256 | bytes 7891790 | solution.py:126
  323.4 1.4 gather_fusion.2
  326.2 1.7 fusion.143
  329.0 2.0 fusion.51
  331.9 95.4 %all-reduce.10.cloned.1.call-done = bf16[128,2048]{1,0:T(8,128)(2,1)} async-done(((bf16[128,2048]{1,0:T(8,128)(2,1)}), bf16[128,2048]{1,0:T(8,128)(2,1)}) %all-reduce.10.cloned.1.call-update) | async-done | bytes 524304 | tf_op jit(solution)/shard_map/psum | solution.py:127
  428.4 2.1 collective-permute-start.17
  431.4 1.2 dynamic-slice_select_fusion.1
  432.6 7.7 %conditional.8 = (bf16[128,2048]{1,0:T(8,128)(2,1)S(1)}) conditional(s32[]{:T(128)} %convert_element_type.217, () %tuple.41, (s32[]{:T(128)}, s32[4,8]{1,0:T(4,128)S(1)}, bf16[16,128,256]{2,1,0:T(8,128)(2,1)S(1)}, s32[4]{0:T(128)S(1)}, bf16[128,2048]{1,0:T(8,128)(2,1)S(1)}, /*index=5*/f32[1,2048]{1,0:T(1,128)S(1)}, ...), branch_computations={%region_19.20_spmd, %region_20.24_spmd} | conditional | flops 204260256 | bytes 7891790 | solution.py:126
  432.7 1.4 gather_fusion.3
  435.4 1.7 fusion.148
  438.2 2.0 fusion.75
  441.1 95.5 %all-reduce.12.cloned.1.call-done = bf16[128,2048]{1,0:T(8,128)(2,1)} async-done(((bf16[128,2048]{1,0:T(8,128)(2,1)}), bf16[128,2048]{1,0:T(8,128)(2,1)}) %all-reduce.12.cloned.1.call-update) | async-done | bytes 524304 | tf_op jit(solution)/shard_map/psum | solution.py:127
  537.8 2.1 collective-permute-start.18
  540.7 1.2 dynamic-slice_select_fusion
  544.5 100.7 %all-reduce.14.cloned.1.call-done = bf16[128,2048]{1,0:T(8,128)(2,1)} async-done(((bf16[128,2048]{1,0:T(8,128)(2,1)}), bf16[128,2048]{1,0:T(8,128)(2,1)}) %all-reduce.14.cloned.1.call-update) | async-done | bytes 524304 | tf_op jit(solution)/shard_map/psum | solution.py:127
  645.2 1.4 fusion.129
  (147 shorter events, 27.4 us)
Async XLA Ops:
  6.5 61.2 %copy-start = (bf16[1,2048,128]{2,1,0:T(8,128)(2,1)S(1)}, bf16[1,2048,128]{2,1,0:T(8,128)(2,1)}, u32[]{:S(2)}) copy-start(bf16[1,2048,128]{2,1,0:T(8,128)(2,1)} %param.28) | copy-start | bytes 1572868
  6.5 63.4 %all-gather.3.cloned.1.call-start = ((), (), s32[]{:S(2)}) async-start(), calls=%async_computation | async-start | bytes 2228224 | tf_op jit(solution)/shard_map/all_gather | solution.py:118
  7.3 102.6 %all-gather.5.cloned.1.call-start = ((), (), s32[]{:S(2)}) async-start(), calls=%async_computation.1 | async-start | bytes 1179648 | tf_op jit(solution)/shard_map/all_gather | solution.py:81
  7.3 4.8 collective-permute-start
  8.9 4.5 collective-permute-start.1
  9.7 58.1 %copy-start.15 = (f32[1,2048]{1,0:T(1,128)S(1)}, f32[1,2048]{1,0:T(1,128)}, u32[]{:S(2)}) copy-start(f32[1,2048]{1,0:T(1,128)} %param.31) | copy-start | bytes 24580
  12.1 7.6 %collective-permute-start.2 = (bf16[256,128]{1,0:T(8,128)(2,1)S(1)}, bf16[256,128]{1,0:T(8,128)(2,1)S(1)}, u32[]{:S(2)}, u32[]{:S(2)}) collective-permute-start(bf16[256,128]{1,0:T(8,128)(2,1)S(1)} %collective-permute-done), channel_id=1, source_target_pairs={{0,8},{8,16},{16,24},{24,32},{32,40},{40,48},{48,56},{56,64},{64,7... | collective-permute-start | bytes 196616 | tf_op jit(solution)/shard_map/ppermute | solution.py:17
  13.4 6.3 collective-permute-start.3
  19.7 8.0 %collective-permute-start.4 = (bf16[256,128]{1,0:T(8,128)(2,1)S(1)}, bf16[256,128]{1,0:T(8,128)(2,1)S(1)}, u32[]{:S(2)}, u32[]{:S(2)}) collective-permute-start(bf16[256,128]{1,0:T(8,128)(2,1)S(1)} %collective-permute-done.2), channel_id=1, source_target_pairs={{0,8},{8,16},{16,24},{24,32},{32,40},{40,48},{48,56},{56,64},{64,7... | collective-permute-start | bytes 196616 | tf_op jit(solution)/shard_map/ppermute | solution.py:17
  19.7 8.0 %collective-permute-start.5 = (bf16[256,128]{1,0:T(8,128)(2,1)S(1)}, bf16[256,128]{1,0:T(8,128)(2,1)S(1)}, u32[]{:S(2)}, u32[]{:S(2)}) collective-permute-start(bf16[256,128]{1,0:T(8,128)(2,1)S(1)} %collective-permute-done.3), channel_id=1, source_target_pairs={{0,120},{8,0},{16,8},{24,16},{32,24},{40,32},{48,40},{56,48},{64,5... | collective-permute-start | bytes 196616 | tf_op jit(solution)/shard_map/ppermute | solution.py:20
  27.7 8.4 %collective-permute-start.6 = (bf16[256,128]{1,0:T(8,128)(2,1)S(1)}, bf16[256,128]{1,0:T(8,128)(2,1)S(1)}, u32[]{:S(2)}, u32[]{:S(2)}) collective-permute-start(bf16[256,128]{1,0:T(8,128)(2,1)S(1)} %collective-permute-done.4), channel_id=1, source_target_pairs={{0,8},{8,16},{16,24},{24,32},{32,40},{40,48},{48,56},{56,64},{64,7... | collective-permute-start | bytes 196616 | tf_op jit(solution)/shard_map/ppermute | solution.py:17
  27.7 8.4 %collective-permute-start.7 = (bf16[256,128]{1,0:T(8,128)(2,1)S(1)}, bf16[256,128]{1,0:T(8,128)(2,1)S(1)}, u32[]{:S(2)}, u32[]{:S(2)}) collective-permute-start(bf16[256,128]{1,0:T(8,128)(2,1)S(1)} %collective-permute-done.5), channel_id=1, source_target_pairs={{0,120},{8,0},{16,8},{24,16},{32,24},{40,32},{48,40},{56,48},{64,5... | collective-permute-start | bytes 196616 | tf_op jit(solution)/shard_map/ppermute | solution.py:20
  36.0 7.4 %collective-permute-start.8 = (bf16[256,128]{1,0:T(8,128)(2,1)S(1)}, bf16[256,128]{1,0:T(8,128)(2,1)S(1)}, u32[]{:S(2)}, u32[]{:S(2)}) collective-permute-start(bf16[256,128]{1,0:T(8,128)(2,1)S(1)} %collective-permute-done.6), channel_id=1, source_target_pairs={{0,8},{8,16},{16,24},{24,32},{32,40},{40,48},{48,56},{56,64},{64,7... | collective-permute-start | bytes 196616 | tf_op jit(solution)/shard_map/ppermute | solution.py:17
  36.0 7.4 %collective-permute-start.9 = (bf16[256,128]{1,0:T(8,128)(2,1)S(1)}, bf16[256,128]{1,0:T(8,128)(2,1)S(1)}, u32[]{:S(2)}, u32[]{:S(2)}) collective-permute-start(bf16[256,128]{1,0:T(8,128)(2,1)S(1)} %collective-permute-done.7), channel_id=1, source_target_pairs={{0,120},{8,0},{16,8},{24,16},{32,24},{40,32},{48,40},{56,48},{64,5... | collective-permute-start | bytes 196616 | tf_op jit(solution)/shard_map/ppermute | solution.py:20
  41.2 27.1 %copy-start.13 = (bf16[1,2048,128]{2,1,0:T(8,128)(2,1)S(1)}, bf16[1,2048,128]{2,1,0:T(8,128)(2,1)}, u32[]{:S(2)}) copy-start(bf16[1,2048,128]{2,1,0:T(8,128)(2,1)} %param.27) | copy-start | bytes 1572868
  43.4 8.7 %collective-permute-start.10 = (bf16[256,128]{1,0:T(8,128)(2,1)S(1)}, bf16[256,128]{1,0:T(8,128)(2,1)S(1)}, u32[]{:S(2)}, u32[]{:S(2)}) collective-permute-start(bf16[256,128]{1,0:T(8,128)(2,1)S(1)} %collective-permute-done.8), channel_id=1, source_target_pairs={{0,8},{8,16},{16,24},{24,32},{32,40},{40,48},{48,56},{56,64},{64,7... | collective-permute-start | bytes 196616 | tf_op jit(solution)/shard_map/ppermute | solution.py:17
  43.4 8.7 %collective-permute-start.11 = (bf16[256,128]{1,0:T(8,128)(2,1)S(1)}, bf16[256,128]{1,0:T(8,128)(2,1)S(1)}, u32[]{:S(2)}, u32[]{:S(2)}) collective-permute-start(bf16[256,128]{1,0:T(8,128)(2,1)S(1)} %collective-permute-done.9), channel_id=1, source_target_pairs={{0,120},{8,0},{16,8},{24,16},{32,24},{40,32},{48,40},{56,48},{64,5... | collective-permute-start | bytes 196616 | tf_op jit(solution)/shard_map/ppermute | solution.py:20
  52.1 8.1 %collective-permute-start.12 = (bf16[256,128]{1,0:T(8,128)(2,1)S(1)}, bf16[256,128]{1,0:T(8,128)(2,1)S(1)}, u32[]{:S(2)}, u32[]{:S(2)}) collective-permute-start(bf16[256,128]{1,0:T(8,128)(2,1)S(1)} %collective-permute-done.10), channel_id=1, source_target_pairs={{0,8},{8,16},{16,24},{24,32},{32,40},{40,48},{48,56},{56,64},{64,7... | collective-permute-start | bytes 196616 | tf_op jit(solution)/shard_map/ppermute | solution.py:17
  52.1 8.1 %collective-permute-start.13 = (bf16[256,128]{1,0:T(8,128)(2,1)S(1)}, bf16[256,128]{1,0:T(8,128)(2,1)S(1)}, u32[]{:S(2)}, u32[]{:S(2)}) collective-permute-start(bf16[256,128]{1,0:T(8,128)(2,1)S(1)} %collective-permute-done.11), channel_id=1, source_target_pairs={{0,120},{8,0},{16,8},{24,16},{32,24},{40,32},{48,40},{56,48},{64,5... | collective-permute-start | bytes 196616 | tf_op jit(solution)/shard_map/ppermute | solution.py:20
  60.2 7.2 %collective-permute-start.14 = (bf16[256,128]{1,0:T(8,128)(2,1)S(1)}, bf16[256,128]{1,0:T(8,128)(2,1)S(1)}, u32[]{:S(2)}, u32[]{:S(2)}) collective-permute-start(bf16[256,128]{1,0:T(8,128)(2,1)S(1)} %collective-permute-done.12), channel_id=1, source_target_pairs={{0,8},{8,16},{16,24},{24,32},{32,40},{40,48},{48,56},{56,64},{64,7... | collective-permute-start | bytes 196616 | tf_op jit(solution)/shard_map/ppermute | solution.py:17
  68.4 41.4 %copy-start.14 = (bf16[1,2048,128]{2,1,0:T(8,128)(2,1)S(1)}, bf16[1,2048,128]{2,1,0:T(8,128)(2,1)}, u32[]{:S(2)}) copy-start(bf16[1,2048,128]{2,1,0:T(8,128)(2,1)} %param.26) | copy-start | bytes 1572868
  68.4 41.4 %copy-start.16 = (f32[1,2048]{1,0:T(1,128)S(1)}, f32[1,2048]{1,0:T(1,128)}, u32[]{:S(2)}) copy-start(f32[1,2048]{1,0:T(1,128)} %param.30) | copy-start | bytes 24580
  68.4 41.4 %copy-start.17 = (s32[4,8]{1,0:T(4,128)S(1)}, s32[4,8]{1,0:T(4,128)}, u32[]{:S(2)}) copy-start(s32[4,8]{1,0:T(4,128)} %param.23) | copy-start | bytes 388
  68.4 41.4 %copy-start.18 = (f32[4,8]{1,0:T(4,128)S(1)}, f32[4,8]{1,0:T(4,128)}, u32[]{:S(2)}) copy-start(f32[4,8]{1,0:T(4,128)} %param.25) | copy-start | bytes 388
  68.4 41.4 %copy-start.19 = (s32[4]{0:T(128)S(1)}, s32[4]{0:T(128)}, u32[]{:S(2)}) copy-start(s32[4]{0:T(128)} %param.24) | copy-start | bytes 52
  69.8 140.8 %all-reduce.6.cloned.1.call-start = ((), (), s32[]{:S(2)}) async-start(), calls=%async_computation.2 | async-start | bytes 1048576 | tf_op jit(solution)/shard_map/psum | solution.py:127
  116.0 0.8 copy-start.2
  116.0 100.0 %copy-start.1 = (bf16[16,128,256]{2,1,0:T(8,128)(2,1)S(1)}, bf16[16,128,256]{2,1,0:T(8,128)(2,1)}, u32[]{:S(2)}) copy-start(bf16[16,128,256]{2,1,0:T(8,128)(2,1)} %all-gather.5.cloned.1.call-done) | copy-start | bytes 3145732
  116.8 201.3 %all-reduce.8.cloned.1.call-start = ((), (), s32[]{:S(2)}) async-start(), calls=%async_computation.3 | async-start | bytes 1048576 | tf_op jit(solution)/shard_map/psum | solution.py:127
  212.0 4.0 copy-start.8
  212.0 2.8 collective-permute-start.15
  216.7 3.1 copy-start.12
  221.9 0.8 copy-start.3
  222.8 204.5 %all-reduce.10.cloned.1.call-start = ((), (), s32[]{:S(2)}) async-start(), calls=%async_computation.4 | async-start | bytes 1048576 | tf_op jit(solution)/shard_map/psum | solution.py:127
  319.3 2.8 collective-permute-start.16
  327.9 0.8 copy-start.10
  331.0 0.8 copy-start.4
  331.8 204.8 %all-reduce.12.cloned.1.call-start = ((), (), s32[]{:S(2)}) async-start(), calls=%async_computation.5 | async-start | bytes 1048576 | tf_op jit(solution)/shard_map/psum | solution.py:127
  428.4 4.1 copy-start.7
  428.4 2.9 collective-permute-start.17
  437.2 0.8 copy-start.11
  440.2 0.8 copy-start.5
  441.0 204.2 %all-reduce.14.cloned.1.call-start = ((), (), s32[]{:S(2)}) async-start(), calls=%async_computation.6 | async-start | bytes 1048576 | tf_op jit(solution)/shard_map/psum | solution.py:127
  537.8 2.9 collective-permute-start.18
  542.0 0.8 copy-start.6
  544.5 100.7 %copy-start.9 = (bf16[1,512,128]{2,1,0:T(8,128)(2,1)}, bf16[1,512,128]{2,1,0:T(8,128)(2,1)S(1)}, u32[]{:S(2)}) copy-start(bf16[1,512,128]{2,1,0:T(8,128)(2,1)S(1)} %fusion.130) | copy-start | bytes 393220
Sparse Core Ops, SparseCore 0:
  9.7 55.9 all-gather.2
  70.0 39.8 all-gather.4
  116.9 93.7 all-reduce.5
  222.9 95.1 all-reduce.7
  332.0 95.2 all-reduce.9
  441.2 95.3 all-reduce.11
  542.9 102.2 all-reduce.13
